TPU v7x, 32 devices: a whole 2x2x4 slice. The times are simulated.
32 devices in a mesh: row: 4 (over x, core), col: 8 (over z, y).
Axes of the slice: x: 2, y: 2, z: 4, core: 2. Of those that a mesh axis runs over, the one named last changes fastest.
Arguments:
- vectors: float32 [512, 4096], P('row', 'col'), may hold values from -6 to 6
- factors: float32 [8, 4, 512, 512], P('col', None, 'row'), may hold values from -1 to 1, as said below
- offsets: int32 [8], replicated, may hold values from 0 to 1
Outputs:
- updated: float32 [512, 4096], P('row', 'col')
Inputs may be any that keep to these rules, and one draw needn't show every extreme that they name: Each factors[c, k] is an orthogonal matrix.
All inputs are finite; a program needn't handle non-finite values.
Results may differ from a plain program's by a relative error of at most 0.00014.
Values sent between devices are 32-bit elements; how exact they have to be, the bound alone decides.
No kernel may reach another device: no remote copies, remote signals or barrier semaphores. Data moves between devices by JAX's collectives and lax.ppermute only.
A program may use at most 64 MiB of HBM per device.

v0:
```python
import jax
import jax.numpy as jnp
from jax import lax
from jax.sharding import PartitionSpec as P


def passed_along(block, axis, distance):
    devices = range(lax.axis_size(axis))
    route = [(i - distance, i) for i in devices if i - distance in devices]
    return lax.ppermute(block, axis, route)


def product(former, latter):
    return jnp.dot(
        former, latter, precision=lax.Precision.HIGHEST, preferred_element_type=jnp.float32
    )


def one_by_one(section, factor_list, stride):
    for factor_no in range(4):
        before = section[:, : factor_no * stride]
        middle = section[:, factor_no * stride : factor_no * stride + 2 * stride]
        beyond = section[:, factor_no * stride + 2 * stride :]
        section = jnp.concatenate([before, product(middle, factor_list[factor_no]), beyond], 1)
    return section


def keep_panel(assembled):
    return assembled


def on_device(vectors, factors, offsets):
    block_cols = vectors.shape[1]
    stride = block_cols // 2
    column = lax.axis_index("col")
    groups = lax.axis_size("col")
    gathered = lax.all_gather(factors, "row", axis=2, tiled=True)
    chain_factors = gathered[0]
    offset = lax.dynamic_index_in_dim(offsets, column, 0, keepdims=False)
    first_col = offset * stride
    identity = jnp.eye(2 * stride, dtype=jnp.float32)
    global_first = column * block_cols + first_col
    factor_list = []
    for factor_no in range(4):
        valid = global_first + factor_no * stride + 2 * stride <= groups * block_cols
        factor_list.append(jnp.where(valid, chain_factors[factor_no], identity))

    def update(assembled):
        section = lax.dynamic_slice_in_dim(assembled, first_col, 5 * stride, 1)
        section = one_by_one(section, factor_list, stride)
        return lax.dynamic_update_slice_in_dim(assembled, section, first_col, 1)

    beside = passed_along(vectors, "col", -1)
    distant = passed_along(vectors, "col", -2)
    assembled = jnp.concatenate([vectors, beside, distant], 1)
    holding = vectors
    changed = assembled
    position = jnp.mod(column, 3)
    leader = column - position
    for tick_num in range(3):
        position = jnp.mod(column - tick_num, 3)
        leader = column - position
        active = leader >= 0
        if tick_num > 0:
            handed = passed_along(changed[:, block_cols:], "col", 1)
            third = passed_along(holding, "col", -2)
            assembled = jnp.concatenate([handed, third], 1)
        changed = lax.cond(active & (position == 0), update, keep_panel, assembled)
        holding = jnp.where(position == 0, changed[:, :block_cols], holding)
    back_near = passed_along(changed[:, block_cols : 2 * block_cols], "col", 1)
    back_far = passed_along(changed[:, 2 * block_cols :], "col", 2)
    chosen = jnp.where(position == 0, holding, jnp.where(position == 1, back_near, back_far))
    return jnp.where(leader >= 0, chosen, holding)


def solution(mesh):
    placed = (P("row", "col"), P("col", None, "row", None), P())
    return jax.shard_map(
        on_device, mesh=mesh, in_specs=placed, out_specs=P("row", "col"), check_vma=False
    )
```

profile of v0, /device:TPU:12, one launch (start us, length us, event | category | flops | bytes accessed | tf_op | source)
XLA Modules:
  0.0 161.8 jit_solution(18137093932071999158)
XLA Ops:
  7.3 2.4 %collective-permute-start = (f32[128,512]{1,0:T(8,128)}, f32[128,512]{1,0:T(8,128)S(1)}, u32[]{:S(2)}, u32[]{:S(2)}) collective-permute-start(f32[128,512]{1,0:T(8,128)} %param.9), channel_id=1, source_target_pairs={{1,0},{2,1},{3,2},{4,3},{5,4},{6,5},{7,6},{9,8},{10,9},{11,10},{12... | collective-permute-start | bytes 786440 | tf_op jit(solution)/shard_map/ppermute | solution.py:10
  9.7 1.9 %collective-permute-start.1 = (f32[128,512]{1,0:T(8,128)}, f32[128,512]{1,0:T(8,128)S(1)}, u32[]{:S(2)}, u32[]{:S(2)}) collective-permute-start(f32[128,512]{1,0:T(8,128)} %param.9), channel_id=1, source_target_pairs={{2,0},{3,1},{4,2},{5,3},{6,4},{7,5},{10,8},{11,9},{12,10},{13,11},... | collective-permute-start | bytes 786440 | tf_op jit(solution)/shard_map/ppermute | solution.py:10
  11.6 1.2 dynamic_slice.13
  14.5 4.9 %collective-permute-done = f32[128,512]{1,0:T(8,128)S(1)} collective-permute-done((f32[128,512]{1,0:T(8,128)}, f32[128,512]{1,0:T(8,128)S(1)}, u32[]{:S(2)}, u32[]{:S(2)}) %collective-permute-start) | collective-permute-done | bytes 262176 | tf_op jit(solution)/shard_map/ppermute | solution.py:10
  20.5 24.0 %all-gather.2.cloned.1.call-done = f32[1,4,512,512]{3,2,1,0:T(8,128)} async-done(((f32[1,4,128,512]{3,2,1,0:T(8,128)}), f32[1,4,512,512]{3,2,1,0:T(8,128)}) %all-gather.2.cloned.1.call-update) | async-done | bytes 4194320 | tf_op jit(solution)/shard_map/all_gather | solution.py:37
  44.5 3.7 %convert_select_fusion = (f32[512,512]{1,0:T(8,128)S(1)}, f32[512,512]{1,0:T(8,128)S(1)}, f32[512,512]{1,0:T(8,128)}, f32[512,512]{1,0:T(8,128)S(1)}) fusion(f32[1,4,512,512]{3,2,1,0:T(8,128)} %all-gather.2.cloned.1.call-done, pred[]{:T(512)S(6)} %le.15, pred[]{:T(512)S(6)} %le.14, pred[]{:T(512)S(6)} %le.13, pred[]{:T(512)S(6)} %le.12), kind=kLoop, calls=%fused_computation.69 | loop fusion | flops 1572864 | bytes 8388612 | tf_op jit(solution)/shard_map/jit(_where)/select_n | solution.py:46
  48.2 17.5 %conditional.3 = (f32[128,1536]{1,0:T(8,128)}) conditional(s32[]{:T(128)} %convert_element_type.20, f32[128,1536]{1,0:T(8,128)} %copy-done, (s32[]{:T(128)}, f32[128,1536]{1,0:T(8,128)}, f32[512,512]{1,0:T(8,128)S(1)}, f32[512,512]{1,0:T(8,128)}, f32[512,512]{1,0:T(8,128)S(1)}, /*index=5*/f32[512,512]{1,0:T(8,128)S(1)}) %tuple.38), branch_computations={%region_0.1_spmd, %region_1.2_spmd} | conditional | flops 1611464704 | bytes 13762710 | solution.py:68
  48.2 2.4 %fusion.6 = f32[128,512]{1,0:T(8,128)} fusion(f32[512,512]{1,0:T(8,128)S(1)} %get-tuple-element.55, f32[128,1536]{1,0:T(8,128)} %get-tuple-element.53, s32[]{:T(128)S(6)} %select_n.67), kind=kOutput, calls=%fused_computation.14 | convolution fusion | flops 402653184 | bytes 1572868 | tf_op jit(solution)/shard_map/cond/branch_1_fun/dot_general | solution.py:14
  50.6 1.2 constant_dynamic-slice_fusion.1
  51.8 2.0 %fusion.4 = f32[128,512]{1,0:T(8,128)S(1)} fusion(f32[512,512]{1,0:T(8,128)} %get-tuple-element.56, f32[128,768]{1,0:T(8,128)S(1)} %constant_dynamic-slice_fusion.1, f32[128,512]{1,0:T(8,128)} %fusion.6), kind=kOutput, calls=%fused_computation.12 | convolution fusion | flops 402718720 | bytes 1966080 | tf_op jit(solution)/shard_map/cond/branch_1_fun/dot_general | solution.py:14
  53.8 1.1 constant_dynamic-slice_fusion
  58.1 1.6 fusion
  59.7 1.9 %pad_maximum_fusion = f32[128,1280]{1,0:T(8,128)} fusion(f32[128,512]{1,0:T(8,128)S(1)} %fusion, f32[128,768]{1,0:T(8,128)} %pad_maximum_fusion.1), kind=kLoop, calls=%fused_computation | loop fusion | flops 163840 | bytes 1310720 | tf_op jit(solution)/shard_map/cond/branch_1_fun/concatenate | solution.py:24
  61.6 4.0 %dynamic_update_slice.6 = f32[128,1536]{1,0:T(8,128)} dynamic-update-slice(f32[128,1536]{1,0:T(8,128)} %get-tuple-element.53, f32[128,1280]{1,0:T(8,128)} %pad_maximum_fusion, s32[]{:T(128)} %constant.26.clone, s32[]{:T(128)S(6)} %select_n.67) | dynamic-update-slice | bytes 1310724 | tf_op jit(solution)/shard_map/cond/branch_1_fun/dynamic_update_slice | solution.py:51
  65.7 1.9 %slice.163 = f32[128,1024]{1,0:T(8,128)} slice(f32[128,1536]{1,0:T(8,128)} %get-tuple-element.77), slice={[0:128], [512:1536]} | slice | bytes 1048576 | tf_op jit(solution)/shard_map/slice | solution.py:65
  67.6 1.9 %collective-permute-start.2 = (f32[128,1024]{1,0:T(8,128)}, f32[128,1024]{1,0:T(8,128)}, u32[]{:S(2)}, u32[]{:S(2)}) collective-permute-start(f32[128,1024]{1,0:T(8,128)} %slice.163), channel_id=1, source_target_pairs={{0,1},{1,2},{2,3},{3,4},{4,5},{5,6},{6,7},{8,9},{9,10},{10,11},{11... | collective-permute-start | bytes 1572872 | tf_op jit(solution)/shard_map/ppermute | solution.py:10
  70.5 1.9 %collective-permute-start.3 = (f32[128,512]{1,0:T(8,128)S(1)}, f32[128,512]{1,0:T(8,128)}, u32[]{:S(2)}, u32[]{:S(2)}) collective-permute-start(f32[128,512]{1,0:T(8,128)S(1)} %slice_select_fusion.2), channel_id=1, source_target_pairs={{2,0},{3,1},{4,2},{5,3},{6,4},{7,5},{10,8},{11,9},{12,10},{13,11},... | collective-permute-start | bytes 786440 | tf_op jit(solution)/shard_map/ppermute | solution.py:10
  72.5 11.4 %collective-permute-done.2 = f32[128,1024]{1,0:T(8,128)} collective-permute-done((f32[128,1024]{1,0:T(8,128)}, f32[128,1024]{1,0:T(8,128)}, u32[]{:S(2)}, u32[]{:S(2)}) %collective-permute-start.2) | collective-permute-done | bytes 524320 | tf_op jit(solution)/shard_map/ppermute | solution.py:10
  83.8 1.9 %constant_dynamic-update-slice_fusion.4 = f32[128,1536]{1,0:T(8,128)} fusion(f32[128,1024]{1,0:T(8,128)} %collective-permute-done.2), kind=kLoop, calls=%fused_computation.86 | loop fusion | bytes 1048576
  85.7 1.7 %constant_dynamic-update-slice_fusion.3 = f32[128,1536]{1,0:T(8,128)} fusion(f32[128,1536]{1,0:T(8,128)} %constant_dynamic-update-slice_fusion.4, f32[128,512]{1,0:T(8,128)} %collective-permute-done.3), kind=kLoop, calls=%fused_computation.85 | loop fusion | bytes 524288 | tf_op jit(solution)/shard_map/concatenate | solution.py:67
  87.4 1.9 %slice.165 = f32[128,1024]{1,0:T(8,128)} slice(f32[128,1536]{1,0:T(8,128)} %get-tuple-element.78), slice={[0:128], [512:1536]} | slice | bytes 1048576 | tf_op jit(solution)/shard_map/slice | solution.py:65
  89.3 20.6 %collective-permute-start.4 = (f32[128,1024]{1,0:T(8,128)}, f32[128,1024]{1,0:T(8,128)}, u32[]{:S(2)}, u32[]{:S(2)}) collective-permute-start(f32[128,1024]{1,0:T(8,128)} %slice.165), channel_id=1, source_target_pairs={{0,1},{1,2},{2,3},{3,4},{4,5},{5,6},{6,7},{8,9},{9,10},{10,11},{11... | collective-permute-start | bytes 1572872 | tf_op jit(solution)/shard_map/ppermute | solution.py:10
  109.9 1.1 slice_select_fusion.1
  111.0 1.9 %collective-permute-start.5 = (f32[128,512]{1,0:T(8,128)S(1)}, f32[128,512]{1,0:T(8,128)}, u32[]{:S(2)}, u32[]{:S(2)}) collective-permute-start(f32[128,512]{1,0:T(8,128)S(1)} %slice_select_fusion.1), channel_id=1, source_target_pairs={{2,0},{3,1},{4,2},{5,3},{6,4},{7,5},{10,8},{11,9},{12,10},{13,11},... | collective-permute-start | bytes 786440 | tf_op jit(solution)/shard_map/ppermute | solution.py:10
  113.0 8.3 %collective-permute-done.4 = f32[128,1024]{1,0:T(8,128)} collective-permute-done((f32[128,1024]{1,0:T(8,128)}, f32[128,1024]{1,0:T(8,128)}, u32[]{:S(2)}, u32[]{:S(2)}) %collective-permute-start.4) | collective-permute-done | bytes 524320 | tf_op jit(solution)/shard_map/ppermute | solution.py:10
  121.2 1.9 %constant_dynamic-update-slice_fusion.6 = f32[128,1536]{1,0:T(8,128)} fusion(f32[128,1024]{1,0:T(8,128)} %collective-permute-done.4), kind=kLoop, calls=%fused_computation.88 | loop fusion | bytes 1048576
  123.1 1.7 %constant_dynamic-update-slice_fusion.5 = f32[128,1536]{1,0:T(8,128)} fusion(f32[128,1536]{1,0:T(8,128)} %constant_dynamic-update-slice_fusion.6, f32[128,512]{1,0:T(8,128)} %collective-permute-done.5), kind=kLoop, calls=%fused_computation.87 | loop fusion | bytes 524288 | tf_op jit(solution)/shard_map/concatenate | solution.py:67
  125.9 5.3 %collective-permute-start.6 = (f32[128,512]{1,0:T(8,128)S(1)}, f32[128,512]{1,0:T(8,128)S(1)}, u32[]{:S(2)}, u32[]{:S(2)}) collective-permute-start(f32[128,512]{1,0:T(8,128)S(1)} %get-tuple-element.76), channel_id=1, source_target_pairs={{0,1},{1,2},{2,3},{3,4},{4,5},{5,6},{6,7},{8,9},{9,10},{10,11},{11... | collective-permute-start | bytes 786440 | tf_op jit(solution)/shard_map/ppermute | solution.py:10
  131.2 12.7 %collective-permute-start.7 = (f32[128,512]{1,0:T(8,128)S(1)}, f32[128,512]{1,0:T(8,128)S(1)}, u32[]{:S(2)}, u32[]{:S(2)}) collective-permute-start(f32[128,512]{1,0:T(8,128)S(1)} %get-tuple-element.75), channel_id=1, source_target_pairs={{0,2},{1,3},{2,4},{3,5},{4,6},{5,7},{8,10},{9,11},{10,12},{11,13},... | collective-permute-start | bytes 786440 | tf_op jit(solution)/shard_map/ppermute | solution.py:10
  143.9 2.5 %collective-permute-done.6 = f32[128,512]{1,0:T(8,128)S(1)} collective-permute-done((f32[128,512]{1,0:T(8,128)S(1)}, f32[128,512]{1,0:T(8,128)S(1)}, u32[]{:S(2)}, u32[]{:S(2)}) %collective-permute-start.6) | collective-permute-done | bytes 262176 | tf_op jit(solution)/shard_map/ppermute | solution.py:10
  146.4 6.8 %collective-permute-done.7 = f32[128,512]{1,0:T(8,128)S(1)} collective-permute-done((f32[128,512]{1,0:T(8,128)S(1)}, f32[128,512]{1,0:T(8,128)S(1)}, u32[]{:S(2)}, u32[]{:S(2)}) %collective-permute-start.7) | collective-permute-done | bytes 262176 | tf_op jit(solution)/shard_map/ppermute | solution.py:10
  153.2 1.8 %select_select_fusion = f32[128,512]{1,0:T(8,128)} fusion(f32[128,512]{1,0:T(8,128)} %copy-done.3, f32[128,1536]{1,0:T(8,128)} %get-tuple-element.79, f32[128,512]{1,0:T(8,128)S(1)} %collective-permute-done.6, f32[128,512]{1,0:T(8,128)S(1)} %collective-permute-done.7, pred[]{:T(512)S(6)} %eq.33, pred[]{:T(512)S(6)} %eq.29, pred[]{:T(512)S(6)} %ge.10), kind=kLoop, calls=%fused_computation.78 | loop fusion | flops 262144 | bytes 1310723 | tf_op jit(solution)/shard_map/jit(_where)/select_n | solution.py:73
  (25 shorter events, 8.0 us)
Async XLA Ops:
  6.5 38.0 %all-gather.2.cloned.1.call-start = ((), (), s32[]{:S(2)}) async-start(), calls=%async_computation | async-start | bytes 5242880 | tf_op jit(solution)/shard_map/all_gather | solution.py:37
  7.3 12.2 %collective-permute-start = (f32[128,512]{1,0:T(8,128)}, f32[128,512]{1,0:T(8,128)S(1)}, u32[]{:S(2)}, u32[]{:S(2)}) collective-permute-start(f32[128,512]{1,0:T(8,128)} %param.9), channel_id=1, source_target_pairs={{1,0},{2,1},{3,2},{4,3},{5,4},{6,5},{7,6},{9,8},{10,9},{11,10},{12... | collective-permute-start | bytes 786440 | tf_op jit(solution)/shard_map/ppermute | solution.py:10
  9.7 9.9 %collective-permute-start.1 = (f32[128,512]{1,0:T(8,128)}, f32[128,512]{1,0:T(8,128)S(1)}, u32[]{:S(2)}, u32[]{:S(2)}) collective-permute-start(f32[128,512]{1,0:T(8,128)} %param.9), channel_id=1, source_target_pairs={{2,0},{3,1},{4,2},{5,3},{6,4},{7,5},{10,8},{11,9},{12,10},{13,11},... | collective-permute-start | bytes 786440 | tf_op jit(solution)/shard_map/ppermute | solution.py:10
  19.6 0.9 copy-start
  50.6 5.7 %slice-start = ((f32[128,512]{1,0:T(8,128)}), f32[128,256]{1,0:T(8,128)S(1)}, s32[]{:S(2)}) async-start(f32[128,512]{1,0:T(8,128)} %fusion.6), calls=%async_computation.1 | async-start | bytes 262144 | tf_op jit(solution)/shard_map/cond/branch_1_fun/slice | solution.py:21
  55.6 0.7 copy-start.1
  67.6 16.3 %collective-permute-start.2 = (f32[128,1024]{1,0:T(8,128)}, f32[128,1024]{1,0:T(8,128)}, u32[]{:S(2)}, u32[]{:S(2)}) collective-permute-start(f32[128,1024]{1,0:T(8,128)} %slice.163), channel_id=1, source_target_pairs={{0,1},{1,2},{2,3},{3,4},{4,5},{5,6},{6,7},{8,9},{9,10},{10,11},{11... | collective-permute-start | bytes 1572872 | tf_op jit(solution)/shard_map/ppermute | solution.py:10
  70.5 17.0 %copy-start.4 = (f32[128,512]{1,0:T(8,128)}, f32[128,512]{1,0:T(8,128)S(1)}, u32[]{:S(2)}) copy-start(f32[128,512]{1,0:T(8,128)S(1)} %slice_select_fusion.2) | copy-start | bytes 786436
  70.5 15.2 %collective-permute-start.3 = (f32[128,512]{1,0:T(8,128)S(1)}, f32[128,512]{1,0:T(8,128)}, u32[]{:S(2)}, u32[]{:S(2)}) collective-permute-start(f32[128,512]{1,0:T(8,128)S(1)} %slice_select_fusion.2), channel_id=1, source_target_pairs={{2,0},{3,1},{4,2},{5,3},{6,4},{7,5},{10,8},{11,9},{12,10},{13,11},... | collective-permute-start | bytes 786440 | tf_op jit(solution)/shard_map/ppermute | solution.py:10
  89.3 31.9 %collective-permute-start.4 = (f32[128,1024]{1,0:T(8,128)}, f32[128,1024]{1,0:T(8,128)}, u32[]{:S(2)}, u32[]{:S(2)}) collective-permute-start(f32[128,1024]{1,0:T(8,128)} %slice.165), channel_id=1, source_target_pairs={{0,1},{1,2},{2,3},{3,4},{4,5},{5,6},{6,7},{8,9},{9,10},{10,11},{11... | collective-permute-start | bytes 1572872 | tf_op jit(solution)/shard_map/ppermute | solution.py:10
  111.0 13.8 %copy-start.3 = (f32[128,512]{1,0:T(8,128)}, f32[128,512]{1,0:T(8,128)S(1)}, u32[]{:S(2)}) copy-start(f32[128,512]{1,0:T(8,128)S(1)} %slice_select_fusion.1) | copy-start | bytes 786436
  111.0 12.1 %collective-permute-start.5 = (f32[128,512]{1,0:T(8,128)S(1)}, f32[128,512]{1,0:T(8,128)}, u32[]{:S(2)}, u32[]{:S(2)}) collective-permute-start(f32[128,512]{1,0:T(8,128)S(1)} %slice_select_fusion.1), channel_id=1, source_target_pairs={{2,0},{3,1},{4,2},{5,3},{6,4},{7,5},{10,8},{11,9},{12,10},{13,11},... | collective-permute-start | bytes 786440 | tf_op jit(solution)/shard_map/ppermute | solution.py:10
  125.9 20.5 %collective-permute-start.6 = (f32[128,512]{1,0:T(8,128)S(1)}, f32[128,512]{1,0:T(8,128)S(1)}, u32[]{:S(2)}, u32[]{:S(2)}) collective-permute-start(f32[128,512]{1,0:T(8,128)S(1)} %get-tuple-element.76), channel_id=1, source_target_pairs={{0,1},{1,2},{2,3},{3,4},{4,5},{5,6},{6,7},{8,9},{9,10},{10,11},{11... | collective-permute-start | bytes 786440 | tf_op jit(solution)/shard_map/ppermute | solution.py:10
  131.2 22.0 %collective-permute-start.7 = (f32[128,512]{1,0:T(8,128)S(1)}, f32[128,512]{1,0:T(8,128)S(1)}, u32[]{:S(2)}, u32[]{:S(2)}) collective-permute-start(f32[128,512]{1,0:T(8,128)S(1)} %get-tuple-element.75), channel_id=1, source_target_pairs={{0,2},{1,3},{2,4},{3,5},{4,6},{5,7},{8,10},{9,11},{10,12},{11,13},... | collective-permute-start | bytes 786440 | tf_op jit(solution)/shard_map/ppermute | solution.py:10
Sparse Core Ops, SparseCore 0:
  8.9 35.5 all-gather.1
where the time goes:
time: 163 us; the launch traced here: 162 us
  waiting for transfers between devices  58.7 us (36%)
  starting transfers between devices  48.6 us (30%)
  local copies, waits for them, and re-layouts  23.2 us (14%)
  between operations  14.3 us (9%)
  other arithmetic  10.3 us (6%)
  matrix products  6.76 us (4%)
    ppermute x8, starting transfers between devices, passed_along(): return lax.ppermute(block, axis, route)  48.6 us
    ppermute x8, waiting for transfers between devices, passed_along(): return lax.ppermute(block, axis, route)  33.9 us
    all_gather x1, waiting for transfers between devices, on_device(): gathered = lax.all_gather(factors, 'row', axis=2, tiled=True)  24 us
    dot_general x4, matrix products, product(): jnp.dot(former, latter, precision=lax.Precision.HIGHEST, preferred_elemen...  6.76 us
    unnamed x10, local copies, waits for them, and re-layouts  5.69 us
    dynamic_update_slice x1, local copies, waits for them, and re-layouts, update(): return lax.dynamic_update_slice_in_dim(assembled, section, first_col, 1)  4.03 us
    slice x2, local copies, waits for them, and re-layouts, on_device(): handed = passed_along(changed[:, block_cols:], 'col', 1)  3.79 us
    select_n x1, other arithmetic, on_device(): factor_list.append(jnp.where(valid, chain_factors[factor_no], identity))  3.68 us
  transfers between devices with their start and end apart: 9, of which 7 were waited for; matrix products, arithmetic and copies ran while one was open for 5% of the time, Pallas kernels for 0%

commit v1 on v0

--- a/solution.py
+++ b/solution.py
@@ -2,6 +2,16 @@
 import jax.numpy as jnp
 from jax import lax
 from jax.sharding import PartitionSpec as P
+
+
+def gather_around(x, axis, dim):
+    ways, here, hop = (lax.axis_size(axis), lax.axis_index(axis), x.shape[dim])
+    shape = [n * ways if d == dim else n for d, n in enumerate(x.shape)]
+    full = lax.dynamic_update_slice_in_dim(jnp.zeros(shape, x.dtype), x, here * hop, axis=dim)
+    for far in range(1, ways):
+        x = lax.ppermute(x, axis, [(d, (d + 1) % ways) for d in range(ways)])
+        full = lax.dynamic_update_slice_in_dim(full, x, (here - far) % ways * hop, axis=dim)
+    return full
 
 
 def passed_along(block, axis, distance):
@@ -34,7 +44,7 @@
     stride = block_cols // 2
     column = lax.axis_index("col")
     groups = lax.axis_size("col")
-    gathered = lax.all_gather(factors, "row", axis=2, tiled=True)
+    gathered = gather_around(factors, "row", 2)
     chain_factors = gathered[0]
     offset = lax.dynamic_index_in_dim(offsets, column, 0, keepdims=False)
     first_col = offset * stride

time: 163 us -> 155 us (0.951); the launches traced: 162 us -> 152 us
  between operations: 14.3 us -> 0.92 us
  local copies, waits for them, and re-layouts: 23.2 us -> 30.7 us
  waiting for transfers between devices: 58.7 us -> 54 us
    ppermute x0 -> x3, waiting for transfers between devices: none -> 29.5 us  [gather_around(): x = lax.ppermute(x, axis, [(d, (d + 1) % ways) for d in range(ways)])]
    all_gather x1 -> x0, waiting for transfers between devices: 24 us -> none  [on_device(): gathered = lax.all_gather(factors, 'row', axis=2, tiled=True)]
    ppermute x8, waiting for transfers between devices: 33.9 us -> 24.5 us  [passed_along(): return lax.ppermute(block, axis, route)]
    dynamic_update_slice x0 -> x4, local copies, waits for them, and re-layouts: none -> 5.56 us  [the longest x3 4.52 us: gather_around(): lax.dynamic_update_slice_in_dim(full, x, (here - far) % ways * hop, axis=...]
    squeeze x0 -> x1, local copies, waits for them, and re-layouts: none -> 2.49 us  [on_device(): chain_factors = gathered[0]]
    unnamed x10 -> x16, local copies, waits for them, and re-layouts: 5.69 us -> 4.81 us
  transfers between devices with their start and end apart: 9 -> 11, of which waited for: 7 -> 7; matrix products, arithmetic and copies ran while one was open for 5% -> 9% of each run, Pallas kernels for 0% -> 0%
where the time goes in v1:
time: 155 us; the launch traced here: 152 us
  waiting for transfers between devices  54 us (35%)
  starting transfers between devices  48.7 us (31%)
  local copies, waits for them, and re-layouts  30.7 us (20%)
  other arithmetic  10.4 us (7%)
  matrix products  6.77 us (4%)
    ppermute x8, starting transfers between devices, passed_along(): return lax.ppermute(block, axis, route)  48.6 us
    ppermute x3, waiting for transfers between devices, gather_around(): x = lax.ppermute(x, axis, [(d, (d + 1) % ways) for d in range(ways)])  29.5 us
    ppermute x8, waiting for transfers between devices, passed_along(): return lax.ppermute(block, axis, route)  24.5 us
    dot_general x4, matrix products, product(): jnp.dot(former, latter, precision=lax.Precision.HIGHEST, preferred_elemen...  6.77 us
    unnamed x16, local copies, waits for them, and re-layouts  4.81 us
    dynamic_update_slice x3, local copies, waits for them, and re-layouts, gather_around(): lax.dynamic_update_slice_in_dim(full, x, (here - far) % ways * hop, axis=...  4.52 us
    dynamic_update_slice x1, local copies, waits for them, and re-layouts, update(): return lax.dynamic_update_slice_in_dim(assembled, section, first_col, 1)  4.04 us
    select_n x1, other arithmetic, on_device(): factor_list.append(jnp.where(valid, chain_factors[factor_no], identity))  3.85 us
  transfers between devices with their start and end apart: 11, of which 7 were waited for; matrix products, arithmetic and copies ran while one was open for 9% of the time, Pallas kernels for 0%

profile of v1, /device:TPU:12, one launch (start us, length us, event | category | flops | bytes accessed | tf_op | source)
XLA Modules:
  0.0 151.6 jit_solution(14011524062047061304)
XLA Ops:
  0.1 14.4 %collective-permute-done.2 = f32[1,4,128,512]{3,2,1,0:T(8,128)S(1)} collective-permute-done((f32[1,4,128,512]{3,2,1,0:T(8,128)}, f32[1,4,128,512]{3,2,1,0:T(8,128)S(1)}, u32[]{:S(2)}, u32[]{:S(2)}) %collective-permute-start.2) | collective-permute-done | bytes 1048608 | tf_op jit(solution)/shard_map/ppermute | solution.py:12
  14.5 2.4 %collective-permute-start = (f32[128,512]{1,0:T(8,128)}, f32[128,512]{1,0:T(8,128)}, u32[]{:S(2)}, u32[]{:S(2)}) collective-permute-start(f32[128,512]{1,0:T(8,128)} %param.9), channel_id=1, source_target_pairs={{1,0},{2,1},{3,2},{4,3},{5,4},{6,5},{7,6},{9,8},{10,9},{11,10},{12... | collective-permute-start | bytes 786440 | tf_op jit(solution)/shard_map/ppermute | solution.py:20
  16.9 1.9 %collective-permute-start.1 = (f32[128,512]{1,0:T(8,128)}, f32[128,512]{1,0:T(8,128)}, u32[]{:S(2)}, u32[]{:S(2)}) collective-permute-start(f32[128,512]{1,0:T(8,128)} %param.9), channel_id=1, source_target_pairs={{2,0},{3,1},{4,2},{5,3},{6,4},{7,5},{10,8},{11,9},{12,10},{13,11},... | collective-permute-start | bytes 786440 | tf_op jit(solution)/shard_map/ppermute | solution.py:20
  18.9 9.9 %collective-permute-done.3 = f32[1,4,128,512]{3,2,1,0:T(8,128)S(1)} collective-permute-done((f32[1,4,128,512]{3,2,1,0:T(8,128)S(1)}, f32[1,4,128,512]{3,2,1,0:T(8,128)S(1)}, u32[]{:S(2)}, u32[]{:S(2)}) %collective-permute-start.3) | collective-permute-done | bytes 1048608 | tf_op jit(solution)/shard_map/ppermute | solution.py:12
  28.7 2.5 %squeeze.25 = f32[4,512,512]{2,1,0:T(8,128)} broadcast(f32[]{:T(128)} %constant.81.clone.1), dimensions={} | broadcast | bytes 4194308 | tf_op jit(solution)/shard_map/squeeze | solution.py:48
  37.8 5.3 %collective-permute-done.4 = f32[1,4,128,512]{3,2,1,0:T(8,128)} collective-permute-done((f32[1,4,128,512]{3,2,1,0:T(8,128)S(1)}, f32[1,4,128,512]{3,2,1,0:T(8,128)}, u32[]{:S(2)}, u32[]{:S(2)}) %collective-permute-start.4) | collective-permute-done | bytes 1048608 | tf_op jit(solution)/shard_map/ppermute | solution.py:12
  43.1 2.3 %bitcast_dynamic-update-slice_fusion = f32[4,512,512]{2,1,0:T(8,128)} fusion(f32[4,512,512]{2,1,0:T(8,128)} %bitcast_dynamic-update-slice_fusion.1, s32[]{:T(128)S(6)} %select_n.130, f32[1,4,128,512]{3,2,1,0:T(8,128)} %collective-permute-done.4), kind=kLoop, calls=%fused_computation.77 | loop fusion | bytes 2097156 | tf_op jit(solution)/shard_map/dynamic_update_slice | solution.py:13
  45.3 3.8 %convert_select_fusion = (f32[512,512]{1,0:T(8,128)S(1)}, f32[512,512]{1,0:T(8,128)S(1)}, f32[512,512]{1,0:T(8,128)}, f32[512,512]{1,0:T(8,128)S(1)}) fusion(f32[4,512,512]{2,1,0:T(8,128)} %bitcast_dynamic-update-slice_fusion, pred[]{:T(512)S(6)} %le.15, pred[]{:T(512)S(6)} %le.14, pred[]{:T(512)S(6)} %le.13, pred[]{:T(512)S(6)} %le.12), kind=kLoop, calls=%fused_computation.69 | loop fusion | flops 1572864 | bytes 8388612 | tf_op jit(solution)/shard_map/jit(_where)/select_n | solution.py:56
  49.2 17.5 %conditional.3 = (f32[128,1536]{1,0:T(8,128)}) conditional(s32[]{:T(128)} %convert_element_type.20, f32[128,1536]{1,0:T(8,128)} %copy-done, (s32[]{:T(128)}, f32[128,1536]{1,0:T(8,128)}, f32[512,512]{1,0:T(8,128)S(1)}, f32[512,512]{1,0:T(8,128)}, f32[512,512]{1,0:T(8,128)S(1)}, /*index=5*/f32[512,512]{1,0:T(8,128)S(1)}) %tuple.36), branch_computations={%region_0.1_spmd, %region_1.2_spmd} | conditional | flops 1611464704 | bytes 13762710 | solution.py:78
  49.2 2.4 %fusion.6 = f32[128,512]{1,0:T(8,128)} fusion(f32[512,512]{1,0:T(8,128)S(1)} %get-tuple-element.55, f32[128,1536]{1,0:T(8,128)} %get-tuple-element.53, s32[]{:T(128)S(6)} %select_n.84), kind=kOutput, calls=%fused_computation.14 | convolution fusion | flops 402653184 | bytes 1572868 | tf_op jit(solution)/shard_map/cond/branch_1_fun/dot_general | solution.py:24
  51.6 1.2 constant_dynamic-slice_fusion.1
  52.8 2.0 %fusion.4 = f32[128,512]{1,0:T(8,128)S(1)} fusion(f32[512,512]{1,0:T(8,128)} %get-tuple-element.56, f32[128,768]{1,0:T(8,128)S(1)} %constant_dynamic-slice_fusion.1, f32[128,512]{1,0:T(8,128)} %fusion.6), kind=kOutput, calls=%fused_computation.12 | convolution fusion | flops 402718720 | bytes 1966080 | tf_op jit(solution)/shard_map/cond/branch_1_fun/dot_general | solution.py:24
  59.1 1.6 %fusion = f32[128,512]{1,0:T(8,128)S(1)} fusion(f32[512,512]{1,0:T(8,128)S(1)} %get-tuple-element.58, f32[128,256]{1,0:T(8,128)S(1)} %constant_dynamic-slice_fusion.2, f32[128,512]{1,0:T(8,128)} %copy-done.1), kind=kOutput, calls=%fused_computation.6 | convolution fusion | flops 402718720 | bytes 1703936 | tf_op jit(solution)/shard_map/cond/branch_1_fun/dot_general | solution.py:24
  60.8 1.9 %pad_maximum_fusion = f32[128,1280]{1,0:T(8,128)} fusion(f32[128,512]{1,0:T(8,128)S(1)} %fusion, f32[128,768]{1,0:T(8,128)} %pad_maximum_fusion.1), kind=kLoop, calls=%fused_computation | loop fusion | flops 163840 | bytes 1310720 | tf_op jit(solution)/shard_map/cond/branch_1_fun/concatenate | solution.py:34
  62.7 4.0 %dynamic_update_slice.18 = f32[128,1536]{1,0:T(8,128)} dynamic-update-slice(f32[128,1536]{1,0:T(8,128)} %get-tuple-element.53, f32[128,1280]{1,0:T(8,128)} %pad_maximum_fusion, s32[]{:T(128)} %constant.66.clone, s32[]{:T(128)S(6)} %select_n.84) | dynamic-update-slice | bytes 1310724 | tf_op jit(solution)/shard_map/cond/branch_1_fun/dynamic_update_slice | solution.py:61
  66.7 1.9 %slice.159 = f32[128,1024]{1,0:T(8,128)} slice(f32[128,1536]{1,0:T(8,128)} %get-tuple-element.77), slice={[0:128], [512:1536]} | slice | bytes 1048576 | tf_op jit(solution)/shard_map/slice | solution.py:75
  68.6 1.9 %collective-permute-start.5 = (f32[128,1024]{1,0:T(8,128)}, f32[128,1024]{1,0:T(8,128)}, u32[]{:S(2)}, u32[]{:S(2)}) collective-permute-start(f32[128,1024]{1,0:T(8,128)} %slice.159), channel_id=1, source_target_pairs={{0,1},{1,2},{2,3},{3,4},{4,5},{5,6},{6,7},{8,9},{9,10},{10,11},{11... | collective-permute-start | bytes 1572872 | tf_op jit(solution)/shard_map/ppermute | solution.py:20
  71.5 1.9 %collective-permute-start.6 = (f32[128,512]{1,0:T(8,128)S(1)}, f32[128,512]{1,0:T(8,128)}, u32[]{:S(2)}, u32[]{:S(2)}) collective-permute-start(f32[128,512]{1,0:T(8,128)S(1)} %slice_select_fusion.2), channel_id=1, source_target_pairs={{2,0},{3,1},{4,2},{5,3},{6,4},{7,5},{10,8},{11,9},{12,10},{13,11},... | collective-permute-start | bytes 786440 | tf_op jit(solution)/shard_map/ppermute | solution.py:20
  73.5 10.2 %collective-permute-done.5 = f32[128,1024]{1,0:T(8,128)} collective-permute-done((f32[128,1024]{1,0:T(8,128)}, f32[128,1024]{1,0:T(8,128)}, u32[]{:S(2)}, u32[]{:S(2)}) %collective-permute-start.5) | collective-permute-done | bytes 524320 | tf_op jit(solution)/shard_map/ppermute | solution.py:20
  83.6 1.9 %constant_dynamic-update-slice_fusion.4 = f32[128,1536]{1,0:T(8,128)} fusion(f32[128,1024]{1,0:T(8,128)} %collective-permute-done.5), kind=kLoop, calls=%fused_computation.90 | loop fusion | bytes 1048576
  85.5 1.7 %constant_dynamic-update-slice_fusion.3 = f32[128,1536]{1,0:T(8,128)} fusion(f32[128,1536]{1,0:T(8,128)} %constant_dynamic-update-slice_fusion.4, f32[128,512]{1,0:T(8,128)} %collective-permute-done.6), kind=kLoop, calls=%fused_computation.89 | loop fusion | bytes 524288 | tf_op jit(solution)/shard_map/concatenate | solution.py:77
  87.3 1.9 %slice.161 = f32[128,1024]{1,0:T(8,128)} slice(f32[128,1536]{1,0:T(8,128)} %get-tuple-element.78), slice={[0:128], [512:1536]} | slice | bytes 1048576 | tf_op jit(solution)/shard_map/slice | solution.py:75
  89.1 20.6 %collective-permute-start.7 = (f32[128,1024]{1,0:T(8,128)}, f32[128,1024]{1,0:T(8,128)}, u32[]{:S(2)}, u32[]{:S(2)}) collective-permute-start(f32[128,1024]{1,0:T(8,128)} %slice.161), channel_id=1, source_target_pairs={{0,1},{1,2},{2,3},{3,4},{4,5},{5,6},{6,7},{8,9},{9,10},{10,11},{11... | collective-permute-start | bytes 1572872 | tf_op jit(solution)/shard_map/ppermute | solution.py:20
  110.8 1.9 %collective-permute-start.8 = (f32[128,512]{1,0:T(8,128)S(1)}, f32[128,512]{1,0:T(8,128)}, u32[]{:S(2)}, u32[]{:S(2)}) collective-permute-start(f32[128,512]{1,0:T(8,128)S(1)} %slice_select_fusion.1), channel_id=1, source_target_pairs={{2,0},{3,1},{4,2},{5,3},{6,4},{7,5},{10,8},{11,9},{12,10},{13,11},... | collective-permute-start | bytes 786440 | tf_op jit(solution)/shard_map/ppermute | solution.py:20
  112.8 7.0 %collective-permute-done.7 = f32[128,1024]{1,0:T(8,128)} collective-permute-done((f32[128,1024]{1,0:T(8,128)}, f32[128,1024]{1,0:T(8,128)}, u32[]{:S(2)}, u32[]{:S(2)}) %collective-permute-start.7) | collective-permute-done | bytes 524320 | tf_op jit(solution)/shard_map/ppermute | solution.py:20
  119.8 1.9 %constant_dynamic-update-slice_fusion.6 = f32[128,1536]{1,0:T(8,128)} fusion(f32[128,1024]{1,0:T(8,128)} %collective-permute-done.7), kind=kLoop, calls=%fused_computation.92 | loop fusion | bytes 1048576
  121.7 1.7 %constant_dynamic-update-slice_fusion.5 = f32[128,1536]{1,0:T(8,128)} fusion(f32[128,1536]{1,0:T(8,128)} %constant_dynamic-update-slice_fusion.6, f32[128,512]{1,0:T(8,128)} %collective-permute-done.8), kind=kLoop, calls=%fused_computation.91 | loop fusion | bytes 524288 | tf_op jit(solution)/shard_map/concatenate | solution.py:77
  124.5 16.0 %collective-permute-start.10 = (f32[128,512]{1,0:T(8,128)S(1)}, f32[128,512]{1,0:T(8,128)S(1)}, u32[]{:S(2)}, u32[]{:S(2)}) collective-permute-start(f32[128,512]{1,0:T(8,128)S(1)} %get-tuple-element.75), channel_id=1, source_target_pairs={{0,2},{1,3},{2,4},{3,5},{4,6},{5,7},{8,10},{9,11},{10,12},{11,13},... | collective-permute-start | bytes 786440 | tf_op jit(solution)/shard_map/ppermute | solution.py:20
  140.5 1.9 %collective-permute-start.9 = (f32[128,512]{1,0:T(8,128)S(1)}, f32[128,512]{1,0:T(8,128)S(1)}, u32[]{:S(2)}, u32[]{:S(2)}) collective-permute-start(f32[128,512]{1,0:T(8,128)S(1)} %get-tuple-element.76), channel_id=1, source_target_pairs={{0,1},{1,2},{2,3},{3,4},{4,5},{5,6},{6,7},{8,9},{9,10},{10,11},{11... | collective-permute-start | bytes 786440 | tf_op jit(solution)/shard_map/ppermute | solution.py:20
  142.5 4.4 %collective-permute-done.10 = f32[128,512]{1,0:T(8,128)S(1)} collective-permute-done((f32[128,512]{1,0:T(8,128)S(1)}, f32[128,512]{1,0:T(8,128)S(1)}, u32[]{:S(2)}, u32[]{:S(2)}) %collective-permute-start.10) | collective-permute-done | bytes 262176 | tf_op jit(solution)/shard_map/ppermute | solution.py:20
  146.9 2.8 %collective-permute-done.9 = f32[128,512]{1,0:T(8,128)S(1)} collective-permute-done((f32[128,512]{1,0:T(8,128)S(1)}, f32[128,512]{1,0:T(8,128)S(1)}, u32[]{:S(2)}, u32[]{:S(2)}) %collective-permute-start.9) | collective-permute-done | bytes 262176 | tf_op jit(solution)/shard_map/ppermute | solution.py:20
  149.7 1.8 %select_select_fusion = f32[128,512]{1,0:T(8,128)} fusion(f32[128,512]{1,0:T(8,128)} %copy-done.5, f32[128,1536]{1,0:T(8,128)} %get-tuple-element.79, f32[128,512]{1,0:T(8,128)S(1)} %collective-permute-done.9, f32[128,512]{1,0:T(8,128)S(1)} %collective-permute-done.10, pred[]{:T(512)S(6)} %eq.36, pred[]{:T(512)S(6)} %eq.32, pred[]{:T(512)S(6)} %ge.10), kind=kLoop, calls=%fused_computation.82 | loop fusion | flops 262144 | bytes 1310723 | tf_op jit(solution)/shard_map/jit(_where)/select_n | solution.py:83
  (39 shorter events, 13.3 us)
Async XLA Ops:
  0.0 31.2 %copy-start.3 = (f32[1,4,128,512]{3,2,1,0:T(8,128)S(1)}, f32[1,4,128,512]{3,2,1,0:T(8,128)}, u32[]{:S(2)}) copy-start(f32[1,4,128,512]{3,2,1,0:T(8,128)} %param.10) | copy-start | bytes 3145732
  0.0 33.5 %copy-start.4 = (f32[128,512]{1,0:T(8,128)S(1)}, f32[128,512]{1,0:T(8,128)}, u32[]{:S(2)}) copy-start(f32[128,512]{1,0:T(8,128)} %param.9) | copy-start | bytes 786436
  0.0 32.3 %copy-start.7 = (s32[8]{0:T(128)S(1)}, s32[8]{0:T(128)}, u32[]{:S(2)}) copy-start(s32[8]{0:T(128)} %param.11) | copy-start | bytes 100
  0.0 14.5 %collective-permute-start.2 = (f32[1,4,128,512]{3,2,1,0:T(8,128)}, f32[1,4,128,512]{3,2,1,0:T(8,128)S(1)}, u32[]{:S(2)}, u32[]{:S(2)}) collective-permute-start(f32[1,4,128,512]{3,2,1,0:T(8,128)} %param.10), channel_id=1, source_target_pairs={{0,8},{8,16},{16,24},{24,0},{1,9},{9,17},{17,25},{25,1},{2,10},{10... | collective-permute-start | bytes 3145736 | tf_op jit(solution)/shard_map/ppermute | solution.py:12
  14.5 14.2 %collective-permute-start.3 = (f32[1,4,128,512]{3,2,1,0:T(8,128)S(1)}, f32[1,4,128,512]{3,2,1,0:T(8,128)S(1)}, u32[]{:S(2)}, u32[]{:S(2)}) collective-permute-start(f32[1,4,128,512]{3,2,1,0:T(8,128)S(1)} %collective-permute-done.2), channel_id=1, source_target_pairs={{0,8},{8,16},{16,24},{24,0},{1,9},{9,17},{17,25},{25,1},{2,10},{10... | collective-permute-start | bytes 3145736 | tf_op jit(solution)/shard_map/ppermute | solution.py:12
  14.5 19.1 %collective-permute-start = (f32[128,512]{1,0:T(8,128)}, f32[128,512]{1,0:T(8,128)}, u32[]{:S(2)}, u32[]{:S(2)}) collective-permute-start(f32[128,512]{1,0:T(8,128)} %param.9), channel_id=1, source_target_pairs={{1,0},{2,1},{3,2},{4,3},{5,4},{6,5},{7,6},{9,8},{10,9},{11,10},{12... | collective-permute-start | bytes 786440 | tf_op jit(solution)/shard_map/ppermute | solution.py:20
  16.9 17.7 %collective-permute-start.1 = (f32[128,512]{1,0:T(8,128)}, f32[128,512]{1,0:T(8,128)}, u32[]{:S(2)}, u32[]{:S(2)}) collective-permute-start(f32[128,512]{1,0:T(8,128)} %param.9), channel_id=1, source_target_pairs={{2,0},{3,1},{4,2},{5,3},{6,4},{7,5},{10,8},{11,9},{12,10},{13,11},... | collective-permute-start | bytes 786440 | tf_op jit(solution)/shard_map/ppermute | solution.py:20
  28.7 14.3 %collective-permute-start.4 = (f32[1,4,128,512]{3,2,1,0:T(8,128)S(1)}, f32[1,4,128,512]{3,2,1,0:T(8,128)}, u32[]{:S(2)}, u32[]{:S(2)}) collective-permute-start(f32[1,4,128,512]{3,2,1,0:T(8,128)S(1)} %collective-permute-done.3), channel_id=1, source_target_pairs={{0,8},{8,16},{16,24},{24,0},{1,9},{9,17},{17,25},{25,1},{2,10},{10... | collective-permute-start | bytes 3145736 | tf_op jit(solution)/shard_map/ppermute | solution.py:12
  35.5 7.5 %copy-start = (f32[128,1536]{1,0:T(8,128)}, f32[128,1536]{1,0:T(8,128)S(1)}, u32[]{:S(2)}) copy-start(f32[128,1536]{1,0:T(8,128)S(1)} %constant_dynamic-update-slice_fusion) | copy-start | bytes 2359300
  51.6 5.8 %slice-start = ((f32[128,512]{1,0:T(8,128)}), f32[128,256]{1,0:T(8,128)S(1)}, s32[]{:S(2)}) async-start(f32[128,512]{1,0:T(8,128)} %fusion.6), calls=%async_computation | async-start | bytes 262144 | tf_op jit(solution)/shard_map/cond/branch_1_fun/slice | solution.py:31
  56.6 0.7 copy-start.1
  68.6 15.0 %collective-permute-start.5 = (f32[128,1024]{1,0:T(8,128)}, f32[128,1024]{1,0:T(8,128)}, u32[]{:S(2)}, u32[]{:S(2)}) collective-permute-start(f32[128,1024]{1,0:T(8,128)} %slice.159), channel_id=1, source_target_pairs={{0,1},{1,2},{2,3},{3,4},{4,5},{5,6},{6,7},{8,9},{9,10},{10,11},{11... | collective-permute-start | bytes 1572872 | tf_op jit(solution)/shard_map/ppermute | solution.py:20
  71.5 15.7 %copy-start.6 = (f32[128,512]{1,0:T(8,128)}, f32[128,512]{1,0:T(8,128)S(1)}, u32[]{:S(2)}) copy-start(f32[128,512]{1,0:T(8,128)S(1)} %slice_select_fusion.2) | copy-start | bytes 786436
  71.5 14.0 %collective-permute-start.6 = (f32[128,512]{1,0:T(8,128)S(1)}, f32[128,512]{1,0:T(8,128)}, u32[]{:S(2)}, u32[]{:S(2)}) collective-permute-start(f32[128,512]{1,0:T(8,128)S(1)} %slice_select_fusion.2), channel_id=1, source_target_pairs={{2,0},{3,1},{4,2},{5,3},{6,4},{7,5},{10,8},{11,9},{12,10},{13,11},... | collective-permute-start | bytes 786440 | tf_op jit(solution)/shard_map/ppermute | solution.py:20
  89.1 30.7 %collective-permute-start.7 = (f32[128,1024]{1,0:T(8,128)}, f32[128,1024]{1,0:T(8,128)}, u32[]{:S(2)}, u32[]{:S(2)}) collective-permute-start(f32[128,1024]{1,0:T(8,128)} %slice.161), channel_id=1, source_target_pairs={{0,1},{1,2},{2,3},{3,4},{4,5},{5,6},{6,7},{8,9},{9,10},{10,11},{11... | collective-permute-start | bytes 1572872 | tf_op jit(solution)/shard_map/ppermute | solution.py:20
  110.8 12.6 %copy-start.5 = (f32[128,512]{1,0:T(8,128)}, f32[128,512]{1,0:T(8,128)S(1)}, u32[]{:S(2)}) copy-start(f32[128,512]{1,0:T(8,128)S(1)} %slice_select_fusion.1) | copy-start | bytes 786436
  110.8 10.9 %collective-permute-start.8 = (f32[128,512]{1,0:T(8,128)S(1)}, f32[128,512]{1,0:T(8,128)}, u32[]{:S(2)}, u32[]{:S(2)}) collective-permute-start(f32[128,512]{1,0:T(8,128)S(1)} %slice_select_fusion.1), channel_id=1, source_target_pairs={{2,0},{3,1},{4,2},{5,3},{6,4},{7,5},{10,8},{11,9},{12,10},{13,11},... | collective-permute-start | bytes 786440 | tf_op jit(solution)/shard_map/ppermute | solution.py:20
  124.5 22.4 %collective-permute-start.10 = (f32[128,512]{1,0:T(8,128)S(1)}, f32[128,512]{1,0:T(8,128)S(1)}, u32[]{:S(2)}, u32[]{:S(2)}) collective-permute-start(f32[128,512]{1,0:T(8,128)S(1)} %get-tuple-element.75), channel_id=1, source_target_pairs={{0,2},{1,3},{2,4},{3,5},{4,6},{5,7},{8,10},{9,11},{10,12},{11,13},... | collective-permute-start | bytes 786440 | tf_op jit(solution)/shard_map/ppermute | solution.py:20
  140.5 9.2 %collective-permute-start.9 = (f32[128,512]{1,0:T(8,128)S(1)}, f32[128,512]{1,0:T(8,128)S(1)}, u32[]{:S(2)}, u32[]{:S(2)}) collective-permute-start(f32[128,512]{1,0:T(8,128)S(1)} %get-tuple-element.76), channel_id=1, source_target_pairs={{0,1},{1,2},{2,3},{3,4},{4,5},{5,6},{6,7},{8,9},{9,10},{10,11},{11... | collective-permute-start | bytes 786440 | tf_op jit(solution)/shard_map/ppermute | solution.py:20
